TPU v7x, 32 devices: a whole 2x2x4 slice. The times are simulated.
32 devices in a mesh: dom: 8 (over z, core), grp: 4 (over y, x).
Axes of the slice: x: 2, y: 2, z: 4, core: 2. Of those that a mesh axis runs over, the one named last changes fastest.
Arguments:
- feats: bfloat16 [8192, 256], P(('dom', 'grp')), may hold values from -6 to 6
- w_self: bfloat16 [256, 256], replicated, may hold values from -0.375 to 0.375
- w_neigh: bfloat16 [256, 256], replicated, may hold values from -0.375 to 0.375
- local_tiles: bfloat16 [64, 3, 128, 128], P(('dom', 'grp')), may hold values from -0.15625 to 0.15625
- local_cols: int32 [64, 3], P(('dom', 'grp')), may hold values from 0 to 7, as said below
- cut_tiles: bfloat16 [64, 10, 128, 128], P(('dom', 'grp')), may hold values from -0.15625 to 0.15625
- cut_src: int32 [64, 10], P(('dom', 'grp')), may hold values from 0 to 7, as said below
- send_block: int32 [32, 8], P(('dom', 'grp')), may hold values from 0 to 1
- send_live: int32 [32, 8], P(('dom', 'grp')), may hold values from 0 to 1, as said below
- cotangent: bfloat16 [8192, 256], P(('dom', 'grp')), may hold values from -0.0625 to 0.0625
Outputs:
- layer_out: bfloat16 [8192, 256], P(('dom', 'grp'))
- grad_self: float32 [256, 256], replicated
- grad_neigh: float32 [256, 256], replicated
Inputs may be any that keep to these rules, and one draw needn't show every extreme that they name: `local_cols`: the 3 column blocks of one row block are distinct. `cut_src`: 0 marks an empty slot; the share of filled slots differs from partition to partition. send_live[e, p] is 1 exactly when some row block of device p * 4 + g (g the position of e) has a cut slot with offset naming e's partition; it is 0 where p is e's own partition.
All inputs are finite; a program needn't handle non-finite values.
Results may differ from a plain program's by a relative error of at most 0.0056.
Values may be sent and summed in bfloat16 or wider, within the bound.
A program may use at most 64 MiB of HBM per device.

v0:
```python
import jax
import jax.numpy as jnp
from jax import lax
from jax.sharding import PartitionSpec as P


def body(
    feats,
    w_self,
    w_neigh,
    local_tiles,
    local_cols,
    cut_tiles,
    cut_src,
    send_block,
    send_live,
    cotangent,
):
    row_blocks = local_tiles.shape[0]
    block_size = local_tiles.shape[2]
    features = feats.shape[1]
    partitions = lax.axis_size("dom")
    own_blocks = feats.reshape(row_blocks, block_size, features)
    gathered = lax.all_gather(feats, "grp", axis=0, tiled=True)
    picked = gathered.reshape(-1, block_size, features)[local_cols]
    aggregate_sum = jnp.einsum(
        "rkij,rkjf->rif", local_tiles, picked, preferred_element_type=jnp.float32
    )
    outgoing = own_blocks[send_block[0]] * send_live[0][:, None, None].astype(jnp.bfloat16)
    received = lax.all_to_all(outgoing, "dom", split_axis=0, concat_axis=0, tiled=True)
    source = (lax.axis_index("dom") + cut_src) % partitions
    remote = received[source]
    aggregate_sum = aggregate_sum + jnp.einsum(
        "rkij,rkjf->rif", cut_tiles, remote, preferred_element_type=jnp.float32
    )
    agg = aggregate_sum.reshape(row_blocks * block_size, features).astype(jnp.bfloat16)
    preact = jnp.dot(feats, w_self, preferred_element_type=jnp.float32) + jnp.dot(
        agg, w_neigh, preferred_element_type=jnp.float32
    )
    sigmoid = jax.nn.sigmoid(preact)
    layer_out = (preact * sigmoid).astype(jnp.bfloat16)
    grad_pre = (cotangent.astype(jnp.float32) * sigmoid * (1.0 + preact * (1.0 - sigmoid))).astype(
        jnp.bfloat16
    )
    grad_own = jnp.dot(feats.T, grad_pre, preferred_element_type=jnp.float32)
    grad_agg = jnp.dot(agg.T, grad_pre, preferred_element_type=jnp.float32)
    stacked = jnp.concatenate([grad_own, grad_agg], axis=0)
    shared = lax.psum_scatter(stacked, "grp", scatter_dimension=0, tiled=True)
    shared = lax.psum(shared, "dom")
    summed = lax.all_gather(shared, "grp", axis=0, tiled=True)
    return (layer_out, summed[:features], summed[features:])


def solution(mesh):
    return jax.shard_map(
        body,
        mesh=mesh,
        in_specs=(
            P(("dom", "grp"), None),
            P(),
            P(),
            P(("dom", "grp"), None, None, None),
            P(("dom", "grp"), None),
            P(("dom", "grp"), None, None, None),
            P(("dom", "grp"), None),
            P(("dom", "grp"), None),
            P(("dom", "grp"), None),
            P(("dom", "grp"), None),
        ),
        out_specs=(P(("dom", "grp"), None), P(), P()),
        check_vma=False,
    )
```

profile of v0, /device:TPU:0, one launch (start us, length us, event | category | flops | bytes accessed | tf_op | source)
XLA Modules:
  0.0 135.9 jit_solution(555693463951138174)
XLA Ops:
  7.2 0.7 fusion.3
  7.9 0.7 convert_bitcast_fusion
  8.6 1.5 %gather_fusion.1 = bf16[8,128,256]{2,1,0:T(8,128)(2,1)S(1)} fusion(bf16[2,128,256]{2,1,0:T(8,128)(2,1)} %bitcast.37, s32[1024]{0:T(1024)S(1)} %pad_clamp_fusion.1), kind=kCustom, calls=%fused_computation.1 | custom fusion | bytes 1048608 | tf_op jit(solution)/shard_map/gather | solution.py:29
  10.1 0.9 broadcast_multiply_fusion
  11.0 6.5 %all-to-all-start = ((bf16[8,128,256]{2,1,0:T(8,128)(2,1)}), bf16[8,128,256]{2,1,0:T(8,128)(2,1)S(1)}, u32[]{:S(2)}, u32[]{:S(2)}) async-start(bf16[8,128,256]{2,1,0:T(8,128)(2,1)} %broadcast_multiply_fusion), calls=%async_computation | async-start | bytes 1048576 | tf_op jit(solution)/shard_map/all_to_all | solution.py:30
  17.6 0.1 reshape.70
  17.6 0.1 reshape.54
  17.7 10.6 %all_gather.6 = bf16[1024,256]{1,0:T(8,128)(2,1)S(1)} all-gather(bf16[256,256]{1,0:T(8,128)(2,1)S(1)} %copy-done.1), channel_id=1, replica_groups=mesh['dom'=8,'grp'=4] {'grp'}, dimensions={0}, use_global_device_ids=true | all-gather | bytes 655360 | tf_op jit(solution)/shard_map/all_gather | solution.py:24
  28.3 0.6 gather_fusion
  28.9 0.2 convolution_bitcast_fusion
  29.2 0.2 fusion.5
  29.4 3.5 %all-to-all-done = bf16[8,128,256]{2,1,0:T(8,128)(2,1)S(1)} async-done(((bf16[8,128,256]{2,1,0:T(8,128)(2,1)}), bf16[8,128,256]{2,1,0:T(8,128)(2,1)S(1)}, u32[]{:S(2)}, u32[]{:S(2)}) %all-to-all-start) | async-done | bytes 524320 | tf_op jit(solution)/shard_map/all_to_all | solution.py:30
  32.8 0.6 gather_fusion.2
  33.5 0.3 fusion.1
  33.9 0.5 copy-done.6
  34.4 0.1 copy-done.7
  34.4 0.9 multiply_convert_fusion
  35.4 0.2 fusion.6
  35.6 0.2 convolution_bitcast_fusion.1
  35.8 0.8 pad_maximum_fusion
  36.8 23.8 %reduce-scatter.2.cloned.1.call-done = f32[128,256]{1,0:T(8,128)} async-done(((f32[512,256]{1,0:T(8,128)}), f32[128,256]{1,0:T(8,128)}) %reduce-scatter.2.cloned.1.call-update) | async-done | bytes 131088 | tf_op jit(solution)/shard_map/reduce_scatter | solution.py:48
  60.6 56.7 %all-reduce.2.cloned.1.call-done = f32[128,256]{1,0:T(8,128)} async-done(((f32[128,256]{1,0:T(8,128)}), f32[128,256]{1,0:T(8,128)}) %all-reduce.2.cloned.1.call-update) | async-done | bytes 131088 | tf_op jit(solution)/shard_map/psum | solution.py:49
  117.2 11.0 %all_gather.7 = f32[512,256]{1,0:T(8,128)S(1)} all-gather(f32[128,256]{1,0:T(8,128)} %all-reduce.2.cloned.1.call-done), channel_id=1, replica_groups=mesh['dom'=8,'grp'=4] {'grp'}, dimensions={0}, use_global_device_ids=true | all-gather | bytes 655360 | tf_op jit(solution)/shard_map/all_gather | solution.py:50
  128.3 0.8 fusion.4
  (23 shorter events, 0.2 us)
Async XLA Ops:
  7.2 26.3 %copy-start = (bf16[2,10,128,128]{3,2,1,0:T(8,128)(2,1)S(1)}, bf16[2,10,128,128]{3,2,1,0:T(8,128)(2,1)}, u32[]{:S(2)}) copy-start(bf16[2,10,128,128]{3,2,1,0:T(8,128)(2,1)} %param.15) | copy-start | bytes 1966084
  10.1 7.5 %copy-start.4 = (s32[2,10]{1,0:T(2,128)S(1)}, s32[2,10]{1,0:T(2,128)}, u32[]{:S(2)}) copy-start(s32[2,10]{1,0:T(2,128)} %param.16) | copy-start | bytes 244
  10.1 7.6 %copy-start.5 = (s32[2,3]{1,0:T(2,128)S(1)}, s32[2,3]{1,0:T(2,128)}, u32[]{:S(2)}) copy-start(s32[2,3]{1,0:T(2,128)} %param.14) | copy-start | bytes 76
  10.1 7.6 %copy-start.1 = (bf16[256,256]{1,0:T(8,128)(2,1)S(1)}, bf16[256,256]{1,0:T(8,128)(2,1)}, u32[]{:S(2)}) copy-start(bf16[256,256]{1,0:T(8,128)(2,1)} %param.10) | copy-start | bytes 393220
  11.0 17.9 %copy-start.2 = (bf16[2,3,128,128]{3,2,1,0:T(8,128)(2,1)S(1)}, bf16[2,3,128,128]{3,2,1,0:T(8,128)(2,1)}, u32[]{:S(2)}) copy-start(bf16[2,3,128,128]{3,2,1,0:T(8,128)(2,1)} %param.13) | copy-start | bytes 589828
  11.0 21.8 %all-to-all-start = ((bf16[8,128,256]{2,1,0:T(8,128)(2,1)}), bf16[8,128,256]{2,1,0:T(8,128)(2,1)S(1)}, u32[]{:S(2)}, u32[]{:S(2)}) async-start(bf16[8,128,256]{2,1,0:T(8,128)(2,1)} %broadcast_multiply_fusion), calls=%async_computation | async-start | bytes 1048576 | tf_op jit(solution)/shard_map/all_to_all | solution.py:30
  17.5 11.7 %copy-start.3 = (bf16[256,256]{1,0:T(8,128)(2,1)S(1)}, bf16[256,256]{1,0:T(8,128)(2,1)}, u32[]{:S(2)}) copy-start(bf16[256,256]{1,0:T(8,128)(2,1)} %param.11) | copy-start | bytes 393220
  17.5 43.1 %reduce-scatter.2.cloned.1.call-start = ((), (), s32[]{:S(2)}) async-start(), calls=%async_computation.2 | async-start | bytes 655360 | tf_op jit(solution)/shard_map/reduce_scatter | solution.py:48
  33.5 0.9 copy-start.6
  33.5 1.0 copy-start.7
  36.7 80.5 %all-reduce.2.cloned.1.call-start = ((), (), s32[]{:S(2)}) async-start(), calls=%async_computation.3 | async-start | bytes 262144 | tf_op jit(solution)/shard_map/psum | solution.py:49
Sparse Core Ops, SparseCore 0:
  36.8 23.6 reduce-scatter.1
  63.0 54.2 all-reduce.1
where the time goes:
time: 136 us
  waiting for transfers between devices  84 us (62%)
  blocking collectives  21.6 us (16%)
  between operations  14.2 us (10%)
  starting transfers between devices  6.54 us (5%)
  local copies, waits for them, and re-layouts  4.3 us (3%)
  other arithmetic  3.17 us (2%)
  matrix products  2.14 us (2%)
    psum x1, waiting for transfers between devices, body(): shared = lax.psum(shared, 'dom')  56.7 us
    reduce_scatter x1, waiting for transfers between devices, body(): shared = lax.psum_scatter(stacked, 'grp', scatter_dimension=0, tiled=True)  23.8 us
    all_gather x1, blocking collectives, body(): summed = lax.all_gather(shared, 'grp', axis=0, tiled=True)  11 us
    all_gather x1, blocking collectives, body(): gathered = lax.all_gather(feats, 'grp', axis=0, tiled=True)  10.6 us
    all_to_all x1, starting transfers between devices, body(): lax.all_to_all(outgoing, 'dom', split_axis=0, concat_axis=0, tiled=True)  6.46 us
    all_to_all x1, waiting for transfers between devices, body(): lax.all_to_all(outgoing, 'dom', split_axis=0, concat_axis=0, tiled=True)  3.46 us
  transfers between devices with their start and end apart: 3, of which 3 were waited for; matrix products, arithmetic and copies ran while one was open for 1% of the time, Pallas kernels for 0%

commit v1 on v0

--- a/solution.py
+++ b/solution.py
@@ -27,7 +27,20 @@
         "rkij,rkjf->rif", local_tiles, picked, preferred_element_type=jnp.float32
     )
     outgoing = own_blocks[send_block[0]] * send_live[0][:, None, None].astype(jnp.bfloat16)
-    received = lax.all_to_all(outgoing, "dom", split_axis=0, concat_axis=0, tiled=True)
+    upper = jax.lax.axis_index("dom")
+    shaped = jax.lax.axis_size("dom")
+    n_now, new = (shaped, upper)
+    block_out = list(outgoing.shape)
+    w1 = outgoing.shape[0] // n_now
+    block_out[0] = w1
+    carry = block_out[0]
+    block_out[0] = carry * n_now
+    received = jnp.zeros(block_out, outgoing.dtype)
+    for d in tuple(range(n_now)):
+        latest = lax.dynamic_slice_in_dim(outgoing, (new ^ d) * w1, w1, axis=0)
+        if d:
+            latest = jax.lax.ppermute(latest, "dom", perm=[(j, j ^ d) for j in range(n_now)])
+        received = lax.dynamic_update_slice_in_dim(received, latest, (new ^ d) * carry, axis=0)
     source = (lax.axis_index("dom") + cut_src) % partitions
     remote = received[source]
     aggregate_sum = aggregate_sum + jnp.einsum(

time: 136 us -> 141 us (1.037)
  starting transfers between devices: 6.54 us -> 9.81 us
  local copies, waits for them, and re-layouts: 4.3 us -> 6.99 us
    ppermute x0 -> x7, starting transfers between devices: none -> 9.73 us  [body(): jax.lax.ppermute(latest, 'dom', perm=[(j, j ^ d) for j in range(n_now)])]
    all_to_all x1 -> x0, starting transfers between devices: 6.46 us -> none  [body(): lax.all_to_all(outgoing, 'dom', split_axis=0, concat_axis=0, tiled=True)]
    ppermute x0 -> x7, waiting for transfers between devices: none -> 3.71 us  [body(): jax.lax.ppermute(latest, 'dom', perm=[(j, j ^ d) for j in range(n_now)])]
    all_to_all x1 -> x0, waiting for transfers between devices: 3.46 us -> none  [body(): lax.all_to_all(outgoing, 'dom', split_axis=0, concat_axis=0, tiled=True)]
    dynamic_update_slice x0 -> x7, local copies, waits for them, and re-layouts: none -> 2.58 us  [body(): lax.dynamic_update_slice_in_dim(received, latest, (new ^ d) * carry, axis=0)]
  transfers between devices with their start and end apart: 3 -> 9, of which waited for: 3 -> 3; matrix products, arithmetic and copies ran while one was open for 1% -> 3% of each run, Pallas kernels for 0% -> 0%
where the time goes in v1:
time: 141 us; the launch traced here: 140 us
  waiting for transfers between devices  83 us (59%)
  blocking collectives  21.6 us (15%)
  between operations  14.3 us (10%)
  starting transfers between devices  9.81 us (7%)
  local copies, waits for them, and re-layouts  6.99 us (5%)
  other arithmetic  2.35 us (2%)
  matrix products  2.13 us (2%)
    psum x1, waiting for transfers between devices, body(): shared = lax.psum(shared, 'dom')  56.7 us
    reduce_scatter x1, waiting for transfers between devices, body(): shared = lax.psum_scatter(stacked, 'grp', scatter_dimension=0, tiled=True)  22.6 us
    all_gather x1, blocking collectives, body(): summed = lax.all_gather(shared, 'grp', axis=0, tiled=True)  11 us
    all_gather x1, blocking collectives, body(): gathered = lax.all_gather(feats, 'grp', axis=0, tiled=True)  10.6 us
    ppermute x7, starting transfers between devices, body(): jax.lax.ppermute(latest, 'dom', perm=[(j, j ^ d) for j in range(n_now)])  9.73 us
    ppermute x7, waiting for transfers between devices, body(): jax.lax.ppermute(latest, 'dom', perm=[(j, j ^ d) for j in range(n_now)])  3.71 us
  transfers between devices with their start and end apart: 9, of which 3 were waited for; matrix products, arithmetic and copies ran while one was open for 3% of the time, Pallas kernels for 0%

profile of v1, /device:TPU:0, one launch (start us, length us, event | category | flops | bytes accessed | tf_op | source)
XLA Modules:
  0.0 140.1 jit_solution(15270233014226268415)
XLA Ops:
  7.3 0.7 fusion.3
  8.0 0.7 convert_bitcast_fusion
  8.6 1.5 %gather_fusion.1 = bf16[8,128,256]{2,1,0:T(8,128)(2,1)S(1)} fusion(bf16[2,128,256]{2,1,0:T(8,128)(2,1)} %bitcast.37, s32[1024]{0:T(1024)S(1)} %pad_clamp_fusion.1), kind=kCustom, calls=%fused_computation.1 | custom fusion | bytes 1048608 | tf_op jit(solution)/shard_map/gather | solution.py:29
  10.4 0.5 collective-permute-start
  10.9 2.7 %collective-permute-start.1 = (bf16[1,128,256]{2,1,0:T(8,128)(2,1)S(1)}, bf16[1,128,256]{2,1,0:T(8,128)(2,1)}, u32[]{:S(2)}, u32[]{:S(2)}) collective-permute-start(bf16[1,128,256]{2,1,0:T(8,128)(2,1)S(1)} %get-tuple-element.10), channel_id=1, source_target_pairs={{0,8},{4,12},{8,0},{12,4},{16,24},{20,28},{24,16},{28,20},{1,9},{5... | collective-permute-start | bytes 196616 | tf_op jit(solution)/shard_map/ppermute | solution.py:42
  13.6 2.8 %collective-permute-start.3 = (bf16[1,128,256]{2,1,0:T(8,128)(2,1)S(1)}, bf16[1,128,256]{2,1,0:T(8,128)(2,1)S(1)}, u32[]{:S(2)}, u32[]{:S(2)}) collective-permute-start(bf16[1,128,256]{2,1,0:T(8,128)(2,1)S(1)} %get-tuple-element.8), channel_id=1, source_target_pairs={{0,16},{4,20},{8,24},{12,28},{16,0},{20,4},{24,8},{28,12},{1,17},{... | collective-permute-start | bytes 196616 | tf_op jit(solution)/shard_map/ppermute | solution.py:42
  16.4 10.6 %all_gather.6 = bf16[1024,256]{1,0:T(8,128)(2,1)S(1)} all-gather(bf16[256,256]{1,0:T(8,128)(2,1)S(1)} %copy-done.1), channel_id=1, replica_groups=mesh['dom'=8,'grp'=4] {'grp'}, dimensions={0}, use_global_device_ids=true | all-gather | bytes 655360 | tf_op jit(solution)/shard_map/all_gather | solution.py:24
  27.4 0.6 gather_fusion
  28.0 0.2 convolution_bitcast_fusion
  28.2 3.7 %collective-permute-start.5 = (bf16[1,128,256]{2,1,0:T(8,128)(2,1)S(1)}, bf16[1,128,256]{2,1,0:T(8,128)(2,1)S(1)}, u32[]{:S(2)}, u32[]{:S(2)}) collective-permute-start(bf16[1,128,256]{2,1,0:T(8,128)(2,1)S(1)} %get-tuple-element.6), channel_id=1, source_target_pairs={{0,24},{4,28},{8,16},{12,20},{16,8},{20,12},{24,0},{28,4},{1,25},{... | collective-permute-start | bytes 196616 | tf_op jit(solution)/shard_map/ppermute | solution.py:42
  31.9 0.8 constant_dynamic-update-slice_fusion.6
  32.8 0.9 constant_dynamic-update-slice_fusion.5
  33.7 0.8 constant_dynamic-update-slice_fusion.4
  34.6 3.7 %collective-permute-done.6 = bf16[1,128,256]{2,1,0:T(8,128)(2,1)S(1)} collective-permute-done((bf16[1,128,256]{2,1,0:T(8,128)(2,1)S(1)}, bf16[1,128,256]{2,1,0:T(8,128)(2,1)S(1)}, u32[]{:S(2)}, u32[]{:S(2)}) %collective-permute-start.6) | collective-permute-done | bytes 65568 | tf_op jit(solution)/shard_map/ppermute | solution.py:42
  38.3 0.6 gather_fusion.2
  39.0 0.3 fusion.1
  39.3 0.5 copy-done.6
  39.9 0.9 multiply_convert_fusion
  40.9 0.2 convolution_bitcast_fusion.1
  41.3 0.8 pad_maximum_fusion
  42.2 22.6 %reduce-scatter.2.cloned.1.call-done = f32[128,256]{1,0:T(8,128)} async-done(((f32[512,256]{1,0:T(8,128)}), f32[128,256]{1,0:T(8,128)}) %reduce-scatter.2.cloned.1.call-update) | async-done | bytes 131088 | tf_op jit(solution)/shard_map/reduce_scatter | solution.py:61
  64.8 56.7 %all-reduce.2.cloned.1.call-done = f32[128,256]{1,0:T(8,128)} async-done(((f32[128,256]{1,0:T(8,128)}), f32[128,256]{1,0:T(8,128)}) %all-reduce.2.cloned.1.call-update) | async-done | bytes 131088 | tf_op jit(solution)/shard_map/psum | solution.py:62
  121.5 11.0 %all_gather.7 = f32[512,256]{1,0:T(8,128)S(1)} all-gather(f32[128,256]{1,0:T(8,128)} %all-reduce.2.cloned.1.call-done), channel_id=1, replica_groups=mesh['dom'=8,'grp'=4] {'grp'}, dimensions={0}, use_global_device_ids=true | all-gather | bytes 655360 | tf_op jit(solution)/shard_map/all_gather | solution.py:63
  132.5 0.8 fusion.4
  (44 shorter events, 1.2 us)
Async XLA Ops:
  7.2 31.8 %copy-start = (bf16[2,10,128,128]{3,2,1,0:T(8,128)(2,1)S(1)}, bf16[2,10,128,128]{3,2,1,0:T(8,128)(2,1)}, u32[]{:S(2)}) copy-start(bf16[2,10,128,128]{3,2,1,0:T(8,128)(2,1)} %param.15) | copy-start | bytes 1966084
  7.2 57.6 %reduce-scatter.2.cloned.1.call-start = ((), (), s32[]{:S(2)}) async-start(), calls=%async_computation.1 | async-start | bytes 655360 | tf_op jit(solution)/shard_map/reduce_scatter | solution.py:61
  10.1 6.3 %copy-start.1 = (bf16[256,256]{1,0:T(8,128)(2,1)S(1)}, bf16[256,256]{1,0:T(8,128)(2,1)}, u32[]{:S(2)}) copy-start(bf16[256,256]{1,0:T(8,128)(2,1)} %param.10) | copy-start | bytes 393220
  10.2 16.7 %copy-start.4 = (s32[2,10]{1,0:T(2,128)S(1)}, s32[2,10]{1,0:T(2,128)}, u32[]{:S(2)}) copy-start(s32[2,10]{1,0:T(2,128)} %param.16) | copy-start | bytes 244
  10.3 16.8 %copy-start.5 = (s32[2,3]{1,0:T(2,128)S(1)}, s32[2,3]{1,0:T(2,128)}, u32[]{:S(2)}) copy-start(s32[2,3]{1,0:T(2,128)} %param.14) | copy-start | bytes 76
  10.3 16.9 %copy-start.3 = (bf16[256,256]{1,0:T(8,128)(2,1)S(1)}, bf16[256,256]{1,0:T(8,128)(2,1)}, u32[]{:S(2)}) copy-start(bf16[256,256]{1,0:T(8,128)(2,1)} %param.11) | copy-start | bytes 393220
  10.3 17.6 %copy-start.2 = (bf16[2,3,128,128]{3,2,1,0:T(8,128)(2,1)S(1)}, bf16[2,3,128,128]{3,2,1,0:T(8,128)(2,1)}, u32[]{:S(2)}) copy-start(bf16[2,3,128,128]{3,2,1,0:T(8,128)(2,1)} %param.13) | copy-start | bytes 589828
  10.4 17.8 %collective-permute-start = (bf16[1,128,256]{2,1,0:T(8,128)(2,1)S(1)}, bf16[1,128,256]{2,1,0:T(8,128)(2,1)}, u32[]{:S(2)}, u32[]{:S(2)}) collective-permute-start(bf16[1,128,256]{2,1,0:T(8,128)(2,1)S(1)} %get-tuple-element.11), channel_id=1, source_target_pairs={{0,4},{4,0},{8,12},{12,8},{16,20},{20,16},{24,28},{28,24},{1,5},{5... | collective-permute-start | bytes 196616 | tf_op jit(solution)/shard_map/ppermute | solution.py:42
  10.9 21.8 %collective-permute-start.1 = (bf16[1,128,256]{2,1,0:T(8,128)(2,1)S(1)}, bf16[1,128,256]{2,1,0:T(8,128)(2,1)}, u32[]{:S(2)}, u32[]{:S(2)}) collective-permute-start(bf16[1,128,256]{2,1,0:T(8,128)(2,1)S(1)} %get-tuple-element.10), channel_id=1, source_target_pairs={{0,8},{4,12},{8,0},{12,4},{16,24},{20,28},{24,16},{28,20},{1,9},{5... | collective-permute-start | bytes 196616 | tf_op jit(solution)/shard_map/ppermute | solution.py:42
  13.6 20.1 %collective-permute-start.2 = (bf16[1,128,256]{2,1,0:T(8,128)(2,1)S(1)}, bf16[1,128,256]{2,1,0:T(8,128)(2,1)}, u32[]{:S(2)}, u32[]{:S(2)}) collective-permute-start(bf16[1,128,256]{2,1,0:T(8,128)(2,1)S(1)} %get-tuple-element.9), channel_id=1, source_target_pairs={{0,12},{4,8},{8,4},{12,0},{16,28},{20,24},{24,20},{28,16},{1,13},{... | collective-permute-start | bytes 196616 | tf_op jit(solution)/shard_map/ppermute | solution.py:42
  13.6 20.9 %collective-permute-start.3 = (bf16[1,128,256]{2,1,0:T(8,128)(2,1)S(1)}, bf16[1,128,256]{2,1,0:T(8,128)(2,1)S(1)}, u32[]{:S(2)}, u32[]{:S(2)}) collective-permute-start(bf16[1,128,256]{2,1,0:T(8,128)(2,1)S(1)} %get-tuple-element.8), channel_id=1, source_target_pairs={{0,16},{4,20},{8,24},{12,28},{16,0},{20,4},{24,8},{28,12},{1,17},{... | collective-permute-start | bytes 196616 | tf_op jit(solution)/shard_map/ppermute | solution.py:42
  16.4 18.1 %collective-permute-start.4 = (bf16[1,128,256]{2,1,0:T(8,128)(2,1)S(1)}, bf16[1,128,256]{2,1,0:T(8,128)(2,1)S(1)}, u32[]{:S(2)}, u32[]{:S(2)}) collective-permute-start(bf16[1,128,256]{2,1,0:T(8,128)(2,1)S(1)} %get-tuple-element.7), channel_id=1, source_target_pairs={{0,20},{4,16},{8,28},{12,24},{16,4},{20,0},{24,12},{28,8},{1,21},{... | collective-permute-start | bytes 196616 | tf_op jit(solution)/shard_map/ppermute | solution.py:42
  28.2 6.3 %collective-permute-start.5 = (bf16[1,128,256]{2,1,0:T(8,128)(2,1)S(1)}, bf16[1,128,256]{2,1,0:T(8,128)(2,1)S(1)}, u32[]{:S(2)}, u32[]{:S(2)}) collective-permute-start(bf16[1,128,256]{2,1,0:T(8,128)(2,1)S(1)} %get-tuple-element.6), channel_id=1, source_target_pairs={{0,24},{4,28},{8,16},{12,20},{16,8},{20,12},{24,0},{28,4},{1,25},{... | collective-permute-start | bytes 196616 | tf_op jit(solution)/shard_map/ppermute | solution.py:42
  32.7 5.5 %collective-permute-start.6 = (bf16[1,128,256]{2,1,0:T(8,128)(2,1)S(1)}, bf16[1,128,256]{2,1,0:T(8,128)(2,1)S(1)}, u32[]{:S(2)}, u32[]{:S(2)}) collective-permute-start(bf16[1,128,256]{2,1,0:T(8,128)(2,1)S(1)} %get-tuple-element.5), channel_id=1, source_target_pairs={{0,28},{4,24},{8,20},{12,16},{16,12},{20,8},{24,4},{28,0},{1,29},{... | collective-permute-start | bytes 196616 | tf_op jit(solution)/shard_map/ppermute | solution.py:42
  38.9 0.9 copy-start.6
  39.0 1.0 copy-start.7
  42.2 79.3 %all-reduce.2.cloned.1.call-start = ((), (), s32[]{:S(2)}) async-start(), calls=%async_computation.2 | async-start | bytes 262144 | tf_op jit(solution)/shard_map/psum | solution.py:62
Sparse Core Ops, SparseCore 0:
  42.3 22.4 reduce-scatter.1
  67.2 54.2 all-reduce.1
